TPU v7x, 32 devices: a whole 2x2x4 slice. The times are simulated.
32 devices in a mesh: row: 4 (over z), col: 8 (over y, x, core).
Axes of the slice: x: 2, y: 2, z: 4, core: 2. Of those that a mesh axis runs over, the one named last changes fastest.
Arguments:
- features: bfloat16 [8, 1024, 256], P('col', 'row'), may hold values from -6 to 6
- weight: bfloat16 [256, 256], replicated, may hold values from -0.375 to 0.375
- cotangent: bfloat16 [8192, 256], P(('row', 'col')), may hold values from -6 to 6
- blk_vals: bfloat16 [4, 8, 192, 128, 128], P('row', 'col'), may hold values from -0.0546875 to 0.0546875
- blk_rows: int32 [4, 8, 192], P('row', 'col'), may hold values from 0 to 15
- blk_cols: int32 [4, 8, 192], P('row', 'col'), may hold values from 0 to 7
- blk_count: int32 [4, 8], P('row', 'col'), may hold values from 24 to 192, as said below
Outputs:
- activated: bfloat16 [8192, 256], P(('row', 'col'))
- grad_weight: float32 [256, 256], replicated
- grad_features: bfloat16 [8, 1024, 256], P('col', 'row')
Inputs may be any that keep to these rules, and one draw needn't show every extreme that they name: Only the first blk_count slots of a panel pair are used; a pair whose row and column node ranges intersect uses all 192, every other pair at most 96.
All inputs are finite; a program needn't handle non-finite values.
Results may differ from a plain program's by a relative error of at most 0.0059.
Values may be sent and summed in bfloat16 or wider, within the bound.
A program may use at most 128 MiB of HBM per device.

v0:
```python
import jax
import jax.numpy as jnp
from jax import lax
from jax.sharding import PartitionSpec as P


def block_terms(values, index, source, live_count, transpose):
    total_slots = values.shape[0]
    group = 64
    width = source.shape[-1]
    side = values.shape[-1]
    if transpose:
        form = "bji,bjf->bif"
    else:
        form = "bij,bjf->bif"

    def one_group(group_index, buffer):
        first = group_index * group
        block_vals = lax.dynamic_slice_in_dim(values, first, group, 0)
        block_ids = lax.dynamic_slice_in_dim(index, first, group, 0)
        picked = jnp.take(source, block_ids, axis=0)
        product = jnp.einsum(form, block_vals, picked, preferred_element_type=jnp.float32)
        alive = first + jnp.arange(group, dtype=jnp.int32) < live_count
        product = jnp.where(alive[:, None, None], product, 0.0)
        return lax.dynamic_update_slice_in_dim(buffer, product, first, 0)

    buffer = jnp.zeros((total_slots, side, width), jnp.float32)
    groups = total_slots // group
    return lax.fori_loop(0, groups, one_group, buffer)


def per_device(features, weight, cotangent, blk_vals, blk_rows, blk_cols, blk_count):
    rows_here = cotangent.shape[0]
    width = cotangent.shape[1]
    side = blk_vals.shape[-1]
    row_blocks = rows_here * lax.axis_size("col") // side
    col_blocks = rows_here * lax.axis_size("row") // side
    values = blk_vals[0, 0]
    row_ids = blk_rows[0, 0]
    col_ids = blk_cols[0, 0]
    live_count = blk_count[0, 0]
    panel = lax.all_gather(features, "row", axis=1, tiled=True)
    source = panel.reshape(col_blocks, side, width)
    products = block_terms(values, col_ids, source, live_count, False)
    partial_rows = jax.ops.segment_sum(products, row_ids, num_segments=row_blocks)
    own_rows = lax.psum_scatter(
        partial_rows.reshape(row_blocks * side, width), "col", scatter_dimension=0, tiled=True
    )
    aggregated = own_rows.astype(jnp.bfloat16)
    pre = jnp.dot(aggregated, weight, preferred_element_type=jnp.float32)
    sigma = jax.nn.sigmoid(pre)
    activated = (pre * sigma).astype(jnp.bfloat16)
    grad_pre = (cotangent.astype(jnp.float32) * sigma * (1.0 + pre * (1.0 - sigma))).astype(
        jnp.bfloat16
    )
    local_weight = lax.dot_general(
        aggregated, grad_pre, (((0,), (0,)), ((), ())), preferred_element_type=jnp.float32
    )
    grad_weight = lax.psum(local_weight, ("row", "col"))
    grad_agg = lax.dot_general(
        grad_pre, weight, (((1,), (1,)), ((), ())), preferred_element_type=jnp.float32
    ).astype(jnp.bfloat16)
    grad_rows = lax.all_gather(grad_agg, "col", axis=0, tiled=True)
    grad_source = grad_rows.reshape(row_blocks, side, width)
    back_products = block_terms(values, row_ids, grad_source, live_count, True)
    partial_cols = jax.ops.segment_sum(back_products, col_ids, num_segments=col_blocks)
    own_cols = lax.psum_scatter(
        partial_cols.reshape(col_blocks * side, width), "row", scatter_dimension=0, tiled=True
    )
    grad_features = own_cols.astype(jnp.bfloat16).reshape(1, rows_here, width)
    return (activated, grad_weight, grad_features)


def solution(mesh):
    return jax.shard_map(
        per_device,
        mesh=mesh,
        in_specs=(
            P("col", "row", None),
            P(),
            P(("row", "col"), None),
            P("row", "col", None, None, None),
            P("row", "col", None),
            P("row", "col", None),
            P("row", "col"),
        ),
        out_specs=(P(("row", "col"), None), P(), P("col", "row", None)),
        check_vma=False,
    )
```

profile of v0, /device:TPU:0, one launch (start us, length us, event | category | flops | bytes accessed | tf_op | source)
XLA Modules:
  0.0 423.9 jit_solution(15833494370647342353)
XLA Ops:
  7.2 0.0 copy-start
  7.2 0.0 reduce-scatter.3.cloned.1.call-start
  7.2 17.6 %all_gather.6 = bf16[1,1024,256]{2,1,0:T(8,128)(2,1)S(1)} all-gather(bf16[1,256,256]{2,1,0:T(8,128)(2,1)} %param.11), channel_id=1, replica_groups=mesh['row'=4,'col'=8] {'row'}, dimensions={1}, use_global_device_ids=true | all-gather | bytes 655360 | tf_op jit(solution)/shard_map/all_gather | solution.py:42
  24.8 11.5 %broadcast.44.clone = f32[192,128,256]{2,1,0:T(8,128)} broadcast(f32[]{:T(128)} %constant.131.clone.1), dimensions={} | broadcast | bytes 25165828 | tf_op jit(solution)/shard_map/broadcast.3
  36.3 32.7 %while.26 = (s32[]{:T(128)}, f32[192,128,256]{2,1,0:T(8,128)}, s32[]{:T(128)}, bf16[192,128,128]{2,1,0:T(8,128)(2,1)}, s32[192]{0:T(256)S(1)}, /*index=5*/bf16[8...) while((s32[]{:T(128)}, f32[192,128,256]{2,1,0:T(8,128)}, s32[]{:T(128)}, ...), condition=%wide.region_1.0_spmd, body=%wide.region_0.1_spmd.sunk | while | flops 541066752 | bytes 23075232 | solution.py:29
  36.3 0.7 compare_and_fusion.4
  37.1 2.8 gather_fusion
  39.8 7.4 %select_dynamic-update-slice_fusion.4 = f32[192,128,256]{2,1,0:T(8,128)} fusion(f32[192,128,256]{2,1,0:T(8,128)} %get-tuple-element.358, s32[]{:T(128)S(6)} %select_n.88, pred[64]{0:T(512)(128)(4,1)S(1)} %get-tuple-element.335, bf16[64,128,256]{2,1,0:T(8,128)(2,1)} %gather_fusion, pred[64]{0:T(512)(128)(4,1)S(1)} %get-tuple-element.337, ...), kind=kOutput, calls=%fused_computation.4.clone.1 | convolution fusion | flops 541065216 | bytes 14681216 | tf_op jit(solution)/shard_map/while/body/eval_jaxpr/bij,bjf->bif/dot_general | solution.py:22
  47.2 0.7 compare_and_fusion.4
  47.9 2.8 gather_fusion
  50.7 7.4 %select_dynamic-update-slice_fusion.4 = f32[192,128,256]{2,1,0:T(8,128)} fusion(f32[192,128,256]{2,1,0:T(8,128)} %get-tuple-element.358, s32[]{:T(128)S(6)} %select_n.88, pred[64]{0:T(512)(128)(4,1)S(1)} %get-tuple-element.335, bf16[64,128,256]{2,1,0:T(8,128)(2,1)} %gather_fusion, pred[64]{0:T(512)(128)(4,1)S(1)} %get-tuple-element.337, ...), kind=kOutput, calls=%fused_computation.4.clone.1 | convolution fusion | flops 541065216 | bytes 14681216 | tf_op jit(solution)/shard_map/while/body/eval_jaxpr/bij,bjf->bif/dot_general | solution.py:22
  58.1 0.7 compare_and_fusion.4
  58.8 2.8 gather_fusion
  61.6 7.4 %select_dynamic-update-slice_fusion.4 = f32[192,128,256]{2,1,0:T(8,128)} fusion(f32[192,128,256]{2,1,0:T(8,128)} %get-tuple-element.358, s32[]{:T(128)S(6)} %select_n.88, pred[64]{0:T(512)(128)(4,1)S(1)} %get-tuple-element.335, bf16[64,128,256]{2,1,0:T(8,128)(2,1)} %gather_fusion, pred[64]{0:T(512)(128)(4,1)S(1)} %get-tuple-element.337, ...), kind=kOutput, calls=%fused_computation.4.clone.1 | convolution fusion | flops 541065216 | bytes 14681216 | tf_op jit(solution)/shard_map/while/body/eval_jaxpr/bij,bjf->bif/dot_general | solution.py:22
  69.0 0.2 broadcast_in_dim.108
  69.2 36.1 %scatter_fusion = f32[16,128,256]{2,1,0:T(8,128)S(1)} fusion(f32[16,128,256]{2,1,0:T(8,128)S(1)} %broadcast_in_dim.108, s32[192]{0:T(256)S(1)} %bitcast.22, f32[192,128,256]{2,1,0:T(8,128)} %get-tuple-element.221), kind=kCustom, calls=%fused_computation.2 | custom fusion | flops 6291456 | bytes 75498240 | tf_op jit(solution)/shard_map/scatter-add | solution.py:45
  105.3 1.3 copy-done.4
  106.6 0.0 reduce-scatter.3.cloned.1.call-update
  106.6 0.0 all-gather.2.cloned.1.call-start
  106.7 43.0 %reduce-scatter.3.cloned.1.call-done = f32[256,256]{1,0:T(8,128)} async-done(((f32[2048,256]{1,0:T(8,128)}), f32[256,256]{1,0:T(8,128)}) %reduce-scatter.3.cloned.1.call-update) | async-done | bytes 262160 | tf_op jit(solution)/shard_map/reduce_scatter | solution.py:46
  149.6 1.9 multiply_convert_fusion
  151.5 0.9 convolution_convert_fusion
  152.4 0.0 all-gather.2.cloned.1.call-update
  152.4 0.0 reduce-scatter.5.cloned.1.call-start
  152.5 8.6 %copy.10 = bf16[1,1,192,128,128]{3,4,2,1,0:T(8,128)(2,1)} copy(bf16[1,1,192,128,128]{4,3,2,1,0:T(8,128)(2,1)} %bitcast.20) | data formatting | bytes 12582912 | tf_op args[3]
  161.0 14.9 %all-gather.2.cloned.1.call-done = bf16[2048,256]{1,0:T(8,128)(2,1)} async-done(((bf16[256,256]{1,0:T(8,128)(2,1)}), bf16[2048,256]{1,0:T(8,128)(2,1)}) %all-gather.2.cloned.1.call-update) | async-done | bytes 1048592 | tf_op jit(solution)/shard_map/all_gather | solution.py:63
  176.0 11.5 %broadcast.44 = f32[192,128,256]{2,1,0:T(8,128)} broadcast(f32[]{:T(128)} %constant.131.clone.1), dimensions={} | broadcast | bytes 25165828 | tf_op jit(solution)/shard_map/broadcast.3
  187.4 32.7 %while.27 = (s32[]{:T(128)}, f32[192,128,256]{2,1,0:T(8,128)}, s32[]{:T(128)}, bf16[192,128,128]{1,2,0:T(8,128)(2,1)}, s32[192]{0:T(256)S(1)}, /*index=5*/bf16[1...) while((s32[]{:T(128)}, f32[192,128,256]{2,1,0:T(8,128)}, s32[]{:T(128)}, ...), condition=%wide.region_6.7_spmd, body=%wide.region_5.6_spmd.sunk | while | flops 541066752 | bytes 23075232 | solution.py:29
  187.4 0.7 compare_and_fusion.5
  188.2 2.8 gather_fusion.1
  191.0 7.4 %select_dynamic-update-slice_fusion.5 = f32[192,128,256]{2,1,0:T(8,128)} fusion(f32[192,128,256]{2,1,0:T(8,128)} %get-tuple-element.388, s32[]{:T(128)S(6)} %select_n.91, pred[64]{0:T(512)(128)(4,1)S(1)} %get-tuple-element.344, bf16[64,128,256]{2,1,0:T(8,128)(2,1)} %gather_fusion.1, pred[64]{0:T(512)(128)(4,1)S(1)} %get-tuple-element.346, ...), kind=kOutput, calls=%fused_computation.16.clone.1 | convolution fusion | flops 541065216 | bytes 14681216 | tf_op jit(solution)/shard_map/while/body/eval_jaxpr/bji,bjf->bif/dot_general | solution.py:22
  198.3 0.7 compare_and_fusion.5
  199.1 2.8 gather_fusion.1
  201.8 7.4 %select_dynamic-update-slice_fusion.5 = f32[192,128,256]{2,1,0:T(8,128)} fusion(f32[192,128,256]{2,1,0:T(8,128)} %get-tuple-element.388, s32[]{:T(128)S(6)} %select_n.91, pred[64]{0:T(512)(128)(4,1)S(1)} %get-tuple-element.344, bf16[64,128,256]{2,1,0:T(8,128)(2,1)} %gather_fusion.1, pred[64]{0:T(512)(128)(4,1)S(1)} %get-tuple-element.346, ...), kind=kOutput, calls=%fused_computation.16.clone.1 | convolution fusion | flops 541065216 | bytes 14681216 | tf_op jit(solution)/shard_map/while/body/eval_jaxpr/bji,bjf->bif/dot_general | solution.py:22
  209.2 0.7 compare_and_fusion.5
  210.0 2.8 gather_fusion.1
  212.7 7.4 %select_dynamic-update-slice_fusion.5 = f32[192,128,256]{2,1,0:T(8,128)} fusion(f32[192,128,256]{2,1,0:T(8,128)} %get-tuple-element.388, s32[]{:T(128)S(6)} %select_n.91, pred[64]{0:T(512)(128)(4,1)S(1)} %get-tuple-element.344, bf16[64,128,256]{2,1,0:T(8,128)(2,1)} %gather_fusion.1, pred[64]{0:T(512)(128)(4,1)S(1)} %get-tuple-element.346, ...), kind=kOutput, calls=%fused_computation.16.clone.1 | convolution fusion | flops 541065216 | bytes 14681216 | tf_op jit(solution)/shard_map/while/body/eval_jaxpr/bji,bjf->bif/dot_general | solution.py:22
  220.1 0.1 broadcast_in_dim.109
  220.2 36.0 %scatter_fusion.1 = f32[8,128,256]{2,1,0:T(8,128)S(1)} fusion(f32[8,128,256]{2,1,0:T(8,128)S(1)} %broadcast_in_dim.109, s32[192]{0:T(256)S(1)} %get-tuple-element.427, f32[192,128,256]{2,1,0:T(8,128)} %get-tuple-element.222), kind=kCustom, calls=%fused_computation.3 | custom fusion | flops 6291456 | bytes 75498240 | tf_op jit(solution)/shard_map/scatter-add | solution.py:66
  256.2 1.0 copy-done.2
  257.2 0.0 reduce-scatter.5.cloned.1.call-update
  257.2 0.0 all-reduce.2.cloned.1.call-start
  257.3 0.9 fusion.18
  258.2 0.0 all-reduce.2.cloned.1.call-update
  258.2 26.4 %reduce-scatter.5.cloned.1.call-done = f32[256,256]{1,0:T(8,128)} async-done(((f32[1024,256]{1,0:T(8,128)}), f32[256,256]{1,0:T(8,128)}) %reduce-scatter.5.cloned.1.call-update) | async-done | bytes 262160 | tf_op jit(solution)/shard_map/reduce_scatter | solution.py:67
  284.7 1.6 convert_bitcast_fusion
  286.3 129.4 %all-reduce.2.cloned.1.call-done = f32[256,256]{1,0:T(8,128)} async-done(((f32[256,256]{1,0:T(8,128)}), f32[256,256]{1,0:T(8,128)}) %all-reduce.2.cloned.1.call-update) | async-done | bytes 262160 | tf_op jit(solution)/shard_map/psum | solution.py:59
  415.7 1.7 copy.30
  (21 shorter events, 0.1 us)
Async XLA Ops:
  7.2 142.5 %copy-start = (bf16[256,256]{1,0:T(8,128)(2,1)S(1)}, bf16[256,256]{1,0:T(8,128)(2,1)}, u32[]{:S(2)}) copy-start(bf16[256,256]{1,0:T(8,128)(2,1)} %param.12) | copy-start | bytes 393220
  7.2 142.5 %reduce-scatter.3.cloned.1.call-start = ((), (), s32[]{:S(2)}) async-start(), calls=%async_computation.2 | async-start | bytes 2359296 | tf_op jit(solution)/shard_map/reduce_scatter | solution.py:46
  24.8 11.5 %copy-start.7 = (s32[1,1,192]{2,1,0:T(1,128)S(1)}, s32[1,1,192]{2,1,0:T(1,128)}, u32[]{:S(2)}) copy-start(s32[1,1,192]{2,1,0:T(1,128)} %param.16) | copy-start | bytes 2308
  36.3 32.9 %copy-start.6 = (s32[1,1,192]{2,1,0:T(1,128)S(1)}, s32[1,1,192]{2,1,0:T(1,128)}, u32[]{:S(2)}) copy-start(s32[1,1,192]{2,1,0:T(1,128)} %param.15) | copy-start | bytes 2308
  69.2 80.4 %copy-start.8 = (bf16[256,256]{1,0:T(8,128)(2,1)S(1)}, bf16[256,256]{1,0:T(8,128)(2,1)}, u32[]{:S(2)}) copy-start(bf16[256,256]{1,0:T(8,128)(2,1)} %param.13) | copy-start | bytes 393220
  105.3 1.3 copy-start.4
  106.6 69.3 %all-gather.2.cloned.1.call-start = ((), (), s32[]{:S(2)}) async-start(), calls=%async_computation.4 | async-start | bytes 1179648 | tf_op jit(solution)/shard_map/all_gather | solution.py:63
  152.4 132.2 %reduce-scatter.5.cloned.1.call-start = ((), (), s32[]{:S(2)}) async-start(), calls=%async_computation.5 | async-start | bytes 1310720 | tf_op jit(solution)/shard_map/reduce_scatter | solution.py:67
  176.0 11.5 %copy-start.3 = (bf16[2048,256]{1,0:T(8,128)(2,1)S(1)}, bf16[2048,256]{1,0:T(8,128)(2,1)}, u32[]{:S(2)}) copy-start(bf16[2048,256]{1,0:T(8,128)(2,1)} %all-gather.2.cloned.1.call-done) | copy-start | bytes 3145732
  220.2 37.1 %copy-start.5 = (f32[256,256]{1,0:T(8,128)S(1)}, f32[256,256]{1,0:T(8,128)}, u32[]{:S(2)}) copy-start(f32[256,256]{1,0:T(8,128)} %reduce-scatter.3.cloned.1.call-done) | copy-start | bytes 786436
  220.2 197.1 %copy-start.1 = (bf16[256,256]{1,0:T(8,128)(2,1)S(1)}, bf16[256,256]{1,0:T(8,128)(2,1)}, u32[]{:S(2)}) copy-start(bf16[256,256]{1,0:T(8,128)(2,1)} %param.12) | copy-start | bytes 393220
  256.2 1.0 copy-start.2
  257.2 158.5 %all-reduce.2.cloned.1.call-start = ((), (), s32[]{:S(2)}) async-start(), calls=%async_computation.3 | async-start | bytes 524288 | tf_op jit(solution)/shard_map/psum | solution.py:59
Sparse Core Ops, SparseCore 0:
  106.7 42.8 reduce-scatter.2
  152.6 23.3 all-gather.1
  257.3 27.2 reduce-scatter.4
  290.6 125.0 all-reduce.1
where the time goes:
time: 425 us; the launch traced here: 424 us
  waiting for transfers between devices  214 us (50%)
  other arithmetic  78.1 us (18%)
  local copies, waits for them, and re-layouts  52.5 us (12%)
  matrix products  47.9 us (11%)
  blocking collectives  17.6 us (4%)
  between operations  13.9 us (3%)
    psum x1, waiting for transfers between devices, per_device(): grad_weight = lax.psum(local_weight, ('row', 'col'))  129 us
    dot_general x6, matrix products, one_group(): jnp.einsum(form, block_vals, picked, preferred_element_type=jnp.float32)  44.3 us
    reduce_scatter x1, waiting for transfers between devices, per_device(): lax.psum_scatter(partial_rows.reshape(row_blocks * side, width), 'col', s...  43 us
    scatter-add x1, other arithmetic, per_device(): jax.ops.segment_sum(products, row_ids, num_segments=row_blocks)  36.1 us
    scatter-add x1, other arithmetic, per_device(): jax.ops.segment_sum(back_products, col_ids, num_segments=col_blocks)  36 us
    reduce_scatter x1, waiting for transfers between devices, per_device(): lax.psum_scatter(partial_cols.reshape(col_blocks * side, width), 'row', s...  26.4 us
    another operation x2, local copies, waits for them, and re-layouts  23 us
    all_gather x1, blocking collectives, per_device(): panel = lax.all_gather(features, 'row', axis=1, tiled=True)  17.6 us
  transfers between devices with their start and end apart: 4, of which 4 were waited for; matrix products, arithmetic and copies ran while one was open for 3% of the time, Pallas kernels for 0%

commit v1 on v0

--- a/solution.py
+++ b/solution.py
@@ -56,7 +56,7 @@
     local_weight = lax.dot_general(
         aggregated, grad_pre, (((0,), (0,)), ((), ())), preferred_element_type=jnp.float32
     )
-    grad_weight = lax.psum(local_weight, ("row", "col"))
+    grad_weight = jnp.sum(lax.all_gather(local_weight, ("row", "col")), axis=0)
     grad_agg = lax.dot_general(
         grad_pre, weight, (((1,), (1,)), ((), ())), preferred_element_type=jnp.float32
     ).astype(jnp.bfloat16)

time: 425 us -> 376 us (0.88)
  waiting for transfers between devices: 214 us -> 162 us
  other arithmetic: 78.1 us -> 82.7 us
    psum x1 -> x0, waiting for transfers between devices: 129 us -> none  [per_device(): grad_weight = lax.psum(local_weight, ('row', 'col'))]
    all_gather x0 -> x1, waiting for transfers between devices: none -> 77.3 us  [per_device(): grad_weight = jnp.sum(lax.all_gather(local_weight, ('row', 'col')), axis=0)]
    reduce_sum x0 -> x1, other arithmetic: none -> 4.63 us  [per_device(): grad_weight = jnp.sum(lax.all_gather(local_weight, ('row', 'col')), axis=0)]
    unnamed x20 -> x19, local copies, waits for them, and re-layouts: 12.6 us -> 11 us
where the time goes in v1:
time: 376 us; the launch traced here: 375 us
  waiting for transfers between devices  162 us (43%)
  other arithmetic  82.7 us (22%)
  local copies, waits for them, and re-layouts  50.9 us (14%)
  matrix products  47.9 us (13%)
  blocking collectives  17.6 us (5%)
  between operations  13.9 us (4%)
    all_gather x1, waiting for transfers between devices, per_device(): grad_weight = jnp.sum(lax.all_gather(local_weight, ('row', 'col')), axis=0)  77.3 us
    dot_general x6, matrix products, one_group(): jnp.einsum(form, block_vals, picked, preferred_element_type=jnp.float32)  44.3 us
    reduce_scatter x1, waiting for transfers between devices, per_device(): lax.psum_scatter(partial_rows.reshape(row_blocks * side, width), 'col', s...  43 us
    scatter-add x1, other arithmetic, per_device(): jax.ops.segment_sum(products, row_ids, num_segments=row_blocks)  36.1 us
    scatter-add x1, other arithmetic, per_device(): jax.ops.segment_sum(back_products, col_ids, num_segments=col_blocks)  36 us
    reduce_scatter x1, waiting for transfers between devices, per_device(): lax.psum_scatter(partial_cols.reshape(col_blocks * side, width), 'row', s...  26.4 us
    another operation x2, local copies, waits for them, and re-layouts  23 us
    all_gather x1, blocking collectives, per_device(): panel = lax.all_gather(features, 'row', axis=1, tiled=True)  17.6 us
  transfers between devices with their start and end apart: 4, of which 4 were waited for; matrix products, arithmetic and copies ran while one was open for 3% of the time, Pallas kernels for 0%

profile of v1, /device:TPU:0, one launch (start us, length us, event | category | flops | bytes accessed | tf_op | source)
XLA Modules:
  0.0 374.8 jit_solution(2304256057935282639)
XLA Ops:
  7.2 0.0 copy-start
  7.2 0.0 reduce-scatter.3.cloned.1.call-start
  7.2 17.6 %all_gather.12 = bf16[1,1024,256]{2,1,0:T(8,128)(2,1)S(1)} all-gather(bf16[1,256,256]{2,1,0:T(8,128)(2,1)} %param.11), channel_id=1, replica_groups=mesh['row'=4,'col'=8] {'row'}, dimensions={1}, use_global_device_ids=true | all-gather | bytes 655360 | tf_op jit(solution)/shard_map/all_gather | solution.py:42
  24.8 11.5 %broadcast.44.clone = f32[192,128,256]{2,1,0:T(8,128)} broadcast(f32[]{:T(128)} %constant.132.clone.1), dimensions={} | broadcast | bytes 25165828 | tf_op jit(solution)/shard_map/broadcast.3
  36.3 32.7 %while.26 = (s32[]{:T(128)}, f32[192,128,256]{2,1,0:T(8,128)}, s32[]{:T(128)}, bf16[192,128,128]{2,1,0:T(8,128)(2,1)}, s32[192]{0:T(256)S(1)}, /*index=5*/bf16[8...) while((s32[]{:T(128)}, f32[192,128,256]{2,1,0:T(8,128)}, s32[]{:T(128)}, ...), condition=%wide.region_1.0_spmd, body=%wide.region_0.1_spmd.sunk | while | flops 541066752 | bytes 23075232 | solution.py:29
  36.3 0.7 compare_and_fusion.4
  37.1 2.8 gather_fusion
  39.8 7.4 %select_dynamic-update-slice_fusion.4 = f32[192,128,256]{2,1,0:T(8,128)} fusion(f32[192,128,256]{2,1,0:T(8,128)} %get-tuple-element.358, s32[]{:T(128)S(6)} %select_n.88, pred[64]{0:T(512)(128)(4,1)S(1)} %get-tuple-element.335, bf16[64,128,256]{2,1,0:T(8,128)(2,1)} %gather_fusion, pred[64]{0:T(512)(128)(4,1)S(1)} %get-tuple-element.337, ...), kind=kOutput, calls=%fused_computation.4.clone.1 | convolution fusion | flops 541065216 | bytes 14681216 | tf_op jit(solution)/shard_map/while/body/eval_jaxpr/bij,bjf->bif/dot_general | solution.py:22
  47.2 0.7 compare_and_fusion.4
  47.9 2.8 gather_fusion
  50.7 7.4 %select_dynamic-update-slice_fusion.4 = f32[192,128,256]{2,1,0:T(8,128)} fusion(f32[192,128,256]{2,1,0:T(8,128)} %get-tuple-element.358, s32[]{:T(128)S(6)} %select_n.88, pred[64]{0:T(512)(128)(4,1)S(1)} %get-tuple-element.335, bf16[64,128,256]{2,1,0:T(8,128)(2,1)} %gather_fusion, pred[64]{0:T(512)(128)(4,1)S(1)} %get-tuple-element.337, ...), kind=kOutput, calls=%fused_computation.4.clone.1 | convolution fusion | flops 541065216 | bytes 14681216 | tf_op jit(solution)/shard_map/while/body/eval_jaxpr/bij,bjf->bif/dot_general | solution.py:22
  58.1 0.7 compare_and_fusion.4
  58.8 2.8 gather_fusion
  61.6 7.4 %select_dynamic-update-slice_fusion.4 = f32[192,128,256]{2,1,0:T(8,128)} fusion(f32[192,128,256]{2,1,0:T(8,128)} %get-tuple-element.358, s32[]{:T(128)S(6)} %select_n.88, pred[64]{0:T(512)(128)(4,1)S(1)} %get-tuple-element.335, bf16[64,128,256]{2,1,0:T(8,128)(2,1)} %gather_fusion, pred[64]{0:T(512)(128)(4,1)S(1)} %get-tuple-element.337, ...), kind=kOutput, calls=%fused_computation.4.clone.1 | convolution fusion | flops 541065216 | bytes 14681216 | tf_op jit(solution)/shard_map/while/body/eval_jaxpr/bij,bjf->bif/dot_general | solution.py:22
  69.0 0.2 broadcast_in_dim.108
  69.2 36.1 %scatter_fusion = f32[16,128,256]{2,1,0:T(8,128)S(1)} fusion(f32[16,128,256]{2,1,0:T(8,128)S(1)} %broadcast_in_dim.108, s32[192]{0:T(256)S(1)} %bitcast.24, f32[192,128,256]{2,1,0:T(8,128)} %get-tuple-element.221), kind=kCustom, calls=%fused_computation.2 | custom fusion | flops 6291456 | bytes 75498240 | tf_op jit(solution)/shard_map/scatter-add | solution.py:45
  105.3 1.3 copy-done.4
  106.6 0.0 reduce-scatter.3.cloned.1.call-update
  106.6 0.0 all-gather.4.cloned.1.call-start
  106.7 43.0 %reduce-scatter.3.cloned.1.call-done = f32[256,256]{1,0:T(8,128)} async-done(((f32[2048,256]{1,0:T(8,128)}), f32[256,256]{1,0:T(8,128)}) %reduce-scatter.3.cloned.1.call-update) | async-done | bytes 262160 | tf_op jit(solution)/shard_map/reduce_scatter | solution.py:46
  149.6 1.9 multiply_convert_fusion
  151.5 0.9 convolution_convert_fusion
  152.4 0.0 all-gather.4.cloned.1.call-update
  152.4 0.0 reduce-scatter.5.cloned.1.call-start
  152.5 8.6 %copy.10 = bf16[1,1,192,128,128]{3,4,2,1,0:T(8,128)(2,1)} copy(bf16[1,1,192,128,128]{4,3,2,1,0:T(8,128)(2,1)} %bitcast.21) | data formatting | bytes 12582912 | tf_op args[3]
  161.0 14.9 %all-gather.4.cloned.1.call-done = bf16[2048,256]{1,0:T(8,128)(2,1)} async-done(((bf16[256,256]{1,0:T(8,128)(2,1)}), bf16[2048,256]{1,0:T(8,128)(2,1)}) %all-gather.4.cloned.1.call-update) | async-done | bytes 1048592 | tf_op jit(solution)/shard_map/all_gather | solution.py:63
  176.0 11.5 %broadcast.44 = f32[192,128,256]{2,1,0:T(8,128)} broadcast(f32[]{:T(128)} %constant.132.clone.1), dimensions={} | broadcast | bytes 25165828 | tf_op jit(solution)/shard_map/broadcast.3
  187.4 32.7 %while.27 = (s32[]{:T(128)}, f32[192,128,256]{2,1,0:T(8,128)}, s32[]{:T(128)}, bf16[192,128,128]{1,2,0:T(8,128)(2,1)}, s32[192]{0:T(256)S(1)}, /*index=5*/bf16[1...) while((s32[]{:T(128)}, f32[192,128,256]{2,1,0:T(8,128)}, s32[]{:T(128)}, ...), condition=%wide.region_6.7_spmd, body=%wide.region_5.6_spmd.sunk | while | flops 541066752 | bytes 23075232 | solution.py:29
  187.4 0.7 compare_and_fusion.5
  188.2 2.8 gather_fusion.1
  191.0 7.4 %select_dynamic-update-slice_fusion.5 = f32[192,128,256]{2,1,0:T(8,128)} fusion(f32[192,128,256]{2,1,0:T(8,128)} %get-tuple-element.388, s32[]{:T(128)S(6)} %select_n.91, pred[64]{0:T(512)(128)(4,1)S(1)} %get-tuple-element.344, bf16[64,128,256]{2,1,0:T(8,128)(2,1)} %gather_fusion.1, pred[64]{0:T(512)(128)(4,1)S(1)} %get-tuple-element.346, ...), kind=kOutput, calls=%fused_computation.16.clone.1 | convolution fusion | flops 541065216 | bytes 14681216 | tf_op jit(solution)/shard_map/while/body/eval_jaxpr/bji,bjf->bif/dot_general | solution.py:22
  198.3 0.7 compare_and_fusion.5
  199.1 2.8 gather_fusion.1
  201.8 7.4 %select_dynamic-update-slice_fusion.5 = f32[192,128,256]{2,1,0:T(8,128)} fusion(f32[192,128,256]{2,1,0:T(8,128)} %get-tuple-element.388, s32[]{:T(128)S(6)} %select_n.91, pred[64]{0:T(512)(128)(4,1)S(1)} %get-tuple-element.344, bf16[64,128,256]{2,1,0:T(8,128)(2,1)} %gather_fusion.1, pred[64]{0:T(512)(128)(4,1)S(1)} %get-tuple-element.346, ...), kind=kOutput, calls=%fused_computation.16.clone.1 | convolution fusion | flops 541065216 | bytes 14681216 | tf_op jit(solution)/shard_map/while/body/eval_jaxpr/bji,bjf->bif/dot_general | solution.py:22
  209.2 0.7 compare_and_fusion.5
  210.0 2.8 gather_fusion.1
  212.7 7.4 %select_dynamic-update-slice_fusion.5 = f32[192,128,256]{2,1,0:T(8,128)} fusion(f32[192,128,256]{2,1,0:T(8,128)} %get-tuple-element.388, s32[]{:T(128)S(6)} %select_n.91, pred[64]{0:T(512)(128)(4,1)S(1)} %get-tuple-element.344, bf16[64,128,256]{2,1,0:T(8,128)(2,1)} %gather_fusion.1, pred[64]{0:T(512)(128)(4,1)S(1)} %get-tuple-element.346, ...), kind=kOutput, calls=%fused_computation.16.clone.1 | convolution fusion | flops 541065216 | bytes 14681216 | tf_op jit(solution)/shard_map/while/body/eval_jaxpr/bji,bjf->bif/dot_general | solution.py:22
  220.1 0.1 broadcast_in_dim.109
  220.2 36.0 %scatter_fusion.1 = f32[8,128,256]{2,1,0:T(8,128)S(1)} fusion(f32[8,128,256]{2,1,0:T(8,128)S(1)} %broadcast_in_dim.109, s32[192]{0:T(256)S(1)} %get-tuple-element.424, f32[192,128,256]{2,1,0:T(8,128)} %get-tuple-element.222), kind=kCustom, calls=%fused_computation.3 | custom fusion | flops 6291456 | bytes 75498240 | tf_op jit(solution)/shard_map/scatter-add | solution.py:66
  256.2 1.1 copy-done.2
  257.3 0.0 reduce-scatter.5.cloned.1.call-update
  257.3 0.0 all-gather.6.cloned.1.call-start
  257.4 0.9 fusion.18
  258.3 0.0 all-gather.6.cloned.1.call-update
  258.3 26.4 %reduce-scatter.5.cloned.1.call-done = f32[256,256]{1,0:T(8,128)} async-done(((f32[1024,256]{1,0:T(8,128)}), f32[256,256]{1,0:T(8,128)}) %reduce-scatter.5.cloned.1.call-update) | async-done | bytes 262160 | tf_op jit(solution)/shard_map/reduce_scatter | solution.py:67
  284.8 1.6 convert_bitcast_fusion
  286.4 77.3 %all-gather.6.cloned.1.call-done = f32[8192,256]{1,0:T(8,128)} async-done(((f32[256,256]{1,0:T(8,128)}), f32[8192,256]{1,0:T(8,128)}) %all-gather.6.cloned.1.call-update) | async-done | bytes 8388624 | tf_op jit(solution)/shard_map/all_gather | solution.py:59
  363.6 4.6 %reduce_sum.9 = f32[256,256]{1,0:T(8,128)} reduce(f32[32,256,256]{2,1,0:T(8,128)} %bitcast.23, f32[]{:T(128)} %constant.132.clone.1), dimensions={0}, to_apply=%region_4.5 | reduce | flops 2031616 | bytes 8650756 | tf_op jit(solution)/shard_map/reduce_sum | solution.py:59
  (21 shorter events, 0.1 us)
Async XLA Ops:
  7.2 142.5 %copy-start = (bf16[256,256]{1,0:T(8,128)(2,1)S(1)}, bf16[256,256]{1,0:T(8,128)(2,1)}, u32[]{:S(2)}) copy-start(bf16[256,256]{1,0:T(8,128)(2,1)} %param.12) | copy-start | bytes 393220
  7.2 142.5 %reduce-scatter.3.cloned.1.call-start = ((), (), s32[]{:S(2)}) async-start(), calls=%async_computation.2 | async-start | bytes 2359296 | tf_op jit(solution)/shard_map/reduce_scatter | solution.py:46
  24.8 11.5 %copy-start.7 = (s32[1,1,192]{2,1,0:T(1,128)S(1)}, s32[1,1,192]{2,1,0:T(1,128)}, u32[]{:S(2)}) copy-start(s32[1,1,192]{2,1,0:T(1,128)} %param.16) | copy-start | bytes 2308
  36.3 32.9 %copy-start.6 = (s32[1,1,192]{2,1,0:T(1,128)S(1)}, s32[1,1,192]{2,1,0:T(1,128)}, u32[]{:S(2)}) copy-start(s32[1,1,192]{2,1,0:T(1,128)} %param.15) | copy-start | bytes 2308
  69.2 80.4 %copy-start.8 = (bf16[256,256]{1,0:T(8,128)(2,1)S(1)}, bf16[256,256]{1,0:T(8,128)(2,1)}, u32[]{:S(2)}) copy-start(bf16[256,256]{1,0:T(8,128)(2,1)} %param.13) | copy-start | bytes 393220
  105.3 1.3 copy-start.4
  106.6 69.3 %all-gather.4.cloned.1.call-start = ((), (), s32[]{:S(2)}) async-start(), calls=%async_computation.3 | async-start | bytes 1179648 | tf_op jit(solution)/shard_map/all_gather | solution.py:63
  152.4 132.3 %reduce-scatter.5.cloned.1.call-start = ((), (), s32[]{:S(2)}) async-start(), calls=%async_computation.4 | async-start | bytes 1310720 | tf_op jit(solution)/shard_map/reduce_scatter | solution.py:67
  176.0 11.5 %copy-start.3 = (bf16[2048,256]{1,0:T(8,128)(2,1)S(1)}, bf16[2048,256]{1,0:T(8,128)(2,1)}, u32[]{:S(2)}) copy-start(bf16[2048,256]{1,0:T(8,128)(2,1)} %all-gather.4.cloned.1.call-done) | copy-start | bytes 3145732
  220.2 37.2 %copy-start.5 = (f32[256,256]{1,0:T(8,128)S(1)}, f32[256,256]{1,0:T(8,128)}, u32[]{:S(2)}) copy-start(f32[256,256]{1,0:T(8,128)} %reduce-scatter.3.cloned.1.call-done) | copy-start | bytes 786436
  220.2 148.1 %copy-start.1 = (bf16[256,256]{1,0:T(8,128)(2,1)S(1)}, bf16[256,256]{1,0:T(8,128)(2,1)}, u32[]{:S(2)}) copy-start(bf16[256,256]{1,0:T(8,128)(2,1)} %param.12) | copy-start | bytes 393220
  256.2 1.1 copy-start.2
  257.3 106.3 %all-gather.6.cloned.1.call-start = ((), (), s32[]{:S(2)}) async-start(), calls=%async_computation.5 | async-start | bytes 8650752 | tf_op jit(solution)/shard_map/all_gather | solution.py:59
Sparse Core Ops, SparseCore 0:
  106.7 42.8 reduce-scatter.2
  152.6 23.3 all-gather.3
  257.4 27.2 reduce-scatter.4
  288.0 75.5 all-gather.5
